TPU v7x, 32 devices: a whole 2x2x4 slice. The times are simulated.
32 devices in a mesh: groups: 2 (over y), rows: 4 (over z), cols: 2 (over x), sub: 2 (over core).
Axes of the slice: x: 2, y: 2, z: 4, core: 2. Of those that a mesh axis runs over, the one named last changes fastest.
Arguments:
- features: bfloat16 [128, 256, 512], P(None, ('groups', 'rows'), ('cols', 'sub')), parts along dimension 1, may hold values from -9 to 9
- guide_image: bfloat16 [3, 256, 512], P(None, ('groups', 'rows'), ('cols', 'sub')), parts along dimension 1, may hold values from 0 to 1
- conv_weight: bfloat16 [3, 3, 64, 128], replicated, may hold values from -0.1875 to 0.1875
- head_weight: float32 [2, 64], replicated, may hold values from -0.75 to 0.75
- pixel_mask: int32 [256, 512], P(('groups', 'rows', 'cols', 'sub')), parts along dimension 0, may hold values 0 or 1
Outputs:
- mixture: float32 [256, 512], P(('groups', 'rows', 'cols', 'sub')), parts along dimension 0
There are 2 independent parts, one for each index of `groups`. A program takes and returns all parts, laid end to end along the dimension named above; an argument that names none is the same for every part. Nothing has to cross between parts.
All inputs are finite; a program needn't handle non-finite values. No bound on the sum of `pixel_mask` on one device may be relied on, other than what follows from the above.
Results may differ from a plain program's by a relative error of at most 0.0003.
Values may be sent and summed in bfloat16 or wider, within the bound.
A program may use at most 64 MiB of HBM per device.

v0:
```python
import jax
import jax.numpy as jnp
from jax import lax
from jax.sharding import PartitionSpec as P

ITERS = 2
RIDGE = 0.05
BASE_WEIGHT = 0.1


def with_halo(cells, sides, width):
    for axis, dim in sides:
        count = lax.axis_size(axis)
        ends = count - 1
        head = lax.slice_in_dim(cells, 0, width, axis=dim)
        tail = lax.slice_in_dim(cells, cells.shape[dim] - width, cells.shape[dim], axis=dim)
        cells = jnp.concatenate(
            [
                lax.ppermute(tail, axis, [(i, (i + 1) % count) for i in range(ends)]),
                cells,
                lax.ppermute(head, axis, [((i + 1) % count, i) for i in range(ends)]),
            ],
            axis=dim,
        )
    return cells


def box_sum(extended):
    vertical = extended[:, :-2, :] + extended[:, 1:-1, :] + extended[:, 2:, :]
    return vertical[:, :, :-2] + vertical[:, :, 1:-1] + vertical[:, :, 2:]


def window_stats(guide_ext):
    average = box_sum(guide_ext) / 9.0
    red_ext, green_ext, blue_ext = (guide_ext[0], guide_ext[1], guide_ext[2])
    products = jnp.stack(
        [
            red_ext * red_ext,
            red_ext * green_ext,
            red_ext * blue_ext,
            green_ext * green_ext,
            green_ext * blue_ext,
            blue_ext * blue_ext,
        ]
    )
    second = box_sum(products) / 9.0
    cov_rr = second[0] - average[0] * average[0] + RIDGE
    cov_rg = second[1] - average[0] * average[1]
    joint_spread_redyellow = second[2] - average[0] * average[2]
    cov_gg = second[3] - average[1] * average[1] + RIDGE
    covariance_green_blue = second[4] - average[1] * average[2]
    cov_bb = second[5] - average[2] * average[2] + RIDGE
    cof_rr = cov_gg * cov_bb - covariance_green_blue * covariance_green_blue
    cof_rg = joint_spread_redyellow * covariance_green_blue - cov_rg * cov_bb
    cof_rb = cov_rg * covariance_green_blue - joint_spread_redyellow * cov_gg
    cof_gg = cov_rr * cov_bb - joint_spread_redyellow * joint_spread_redyellow
    cofactor_green_blue = cov_rg * joint_spread_redyellow - cov_rr * covariance_green_blue
    cof_bb = cov_rr * cov_gg - cov_rg * cov_rg
    determinant = cov_rr * cof_rr + cov_rg * cof_rg + joint_spread_redyellow * cof_rb
    inverse = jnp.stack([cof_rr, cof_rg, cof_rb, cof_gg, cofactor_green_blue, cof_bb]) / determinant
    return (average, inverse)


def coefficients(field_ext, guide_ext, average, inverse):
    field_box = box_sum(field_ext)[0] / 9.0
    crossed = box_sum(guide_ext * field_ext) / 9.0 - average * field_box
    slope_r = inverse[0] * crossed[0] + inverse[1] * crossed[1] + inverse[2] * crossed[2]
    slope_g = inverse[1] * crossed[0] + inverse[3] * crossed[1] + inverse[4] * crossed[2]
    gradient_coefficient_third = (
        inverse[2] * crossed[0] + inverse[4] * crossed[1] + inverse[5] * crossed[2]
    )
    offset = field_box - (
        slope_r * average[0] + slope_g * average[1] + gradient_coefficient_third * average[2]
    )
    return jnp.stack([slope_r, slope_g, gradient_coefficient_third, offset])


def apply_operator(field_map, coef_ext, guide_local_tile, weights):
    summed = box_sum(coef_ext)
    smooth = (
        summed[0] * guide_local_tile[0]
        + summed[1] * guide_local_tile[1]
        + summed[2] * guide_local_tile[2]
        + summed[3]
    )
    return 9.0 * field_map - smooth + weights * field_map


def head_maps(extended, conv_weight, head_weight, height, columns):
    channels = extended.shape[0]
    accumulated = jnp.zeros((conv_weight.shape[2], height * columns), jnp.float32)
    for shift_r in range(3):
        for shift_c in range(3):
            window_cell_count = extended[
                :, shift_r : shift_r + height, shift_c : shift_c + columns
            ].reshape(channels, height * columns)
            accumulated = accumulated + jnp.dot(
                conv_weight[shift_r, shift_c], window_cell_count, preferred_element_type=jnp.float32
            )
    hidden = jnp.maximum(accumulated, 0.0)
    logits = jnp.dot(head_weight, hidden, precision=lax.Precision.HIGHEST)
    seed_map = jax.nn.sigmoid(logits[0])
    certainty = jax.nn.softplus(logits[1])
    return jnp.stack([seed_map, certainty]).reshape(2, height, columns)


def pad_columns(stack):
    return jnp.pad(stack, ((0, 0), (0, 0), (1, 1)))


def strip_rim(stack):
    return pad_columns(with_halo(stack, ((("rows", "cols", "sub"), 1),), 1))


def global_sums(values):
    return lax.psum((values[0], values[1]), ("rows", "cols", "sub"))


def on_device(features, guide_image, conv_weight, head_weight, pixel_mask):
    tile_rows, tile_cols = (features.shape[1], features.shape[2])
    outgoing = (features, guide_image)
    rimmed = (
        with_halo(outgoing[0], (("rows", 1), (("cols", "sub"), 2)), 1),
        with_halo(outgoing[1], (("rows", 1), (("cols", "sub"), 2)), 1),
    )
    predictor_result = head_maps(rimmed[0], conv_weight, head_weight, tile_rows, tile_cols)
    guide_float = guide_image.astype(jnp.float32)
    tile_average, tile_inverse_matrix = window_stats(rimmed[1].astype(jnp.float32))
    stacked = jnp.concatenate([predictor_result, guide_float, tile_average, tile_inverse_matrix])
    strips = lax.all_to_all(stacked, ("cols", "sub"), split_axis=1, concat_axis=2, tiled=True)
    seed_map = strips[0]
    certainty = strips[1]
    guide_local_tile = strips[2:5]
    guide_ext = strip_rim(guide_local_tile)
    average, inverse = (strips[5:8], strips[8:14])
    weights = BASE_WEIGHT + pixel_mask.astype(jnp.float32) * certainty

    def operate(field_map):
        field_ext = strip_rim(field_map[None])
        coef = coefficients(field_ext, guide_ext, average, inverse)
        coef_ext = strip_rim(coef)
        return apply_operator(field_map, coef_ext, guide_local_tile, weights)

    mixture = seed_map
    residual = weights * seed_map - operate(seed_map)
    image_dir = operate(residual)
    norm_now, product = global_sums((jnp.sum(residual * residual), jnp.sum(residual * image_dir)))
    step_size = norm_now / product
    direction, along = (residual, image_dir)
    for iteration in range(ITERS):
        mixture = mixture + step_size * direction
        residual = residual - step_size * along
        if iteration + 1 < ITERS:
            image_dir = operate(residual)
            norm_next, product = global_sums(
                (jnp.sum(residual * residual), jnp.sum(residual * image_dir))
            )
            ratio = norm_next / norm_now
            step_size = norm_next / (product - ratio * norm_next / step_size)
            direction = residual + ratio * direction
            along = image_dir + ratio * along
            norm_now = norm_next
    return mixture


def solution(mesh):
    return jax.shard_map(
        on_device,
        mesh=mesh,
        in_specs=(
            P(None, ("groups", "rows"), ("cols", "sub")),
            P(None, ("groups", "rows"), ("cols", "sub")),
            P(),
            P(),
            P(("groups", "rows", "cols", "sub"), None),
        ),
        out_specs=P(("groups", "rows", "cols", "sub"), None),
        check_vma=False,
    )
```

profile of v0, /device:TPU:0, one launch (start us, length us, event | category | flops | bytes accessed | tf_op | source)
XLA Modules:
  0.0 178.0 jit_solution(652070751891009587)
XLA Ops:
  0.8 4.9 %collective-permute-start.4 = (bf16[3,1,128]{2,1,0:T(2,128)(2,1)S(1)}, bf16[3,1,128]{2,1,0:T(2,128)(2,1)S(1)}, u32[]{:S(2)}, u32[]{:S(2)}) collective-permute-start(bf16[3,1,128]{2,1,0:T(2,128)(2,1)S(1)} %get-tuple-element.77), channel_id=1, source_target_pairs={{0,4},{4,8},{8,12},{1,5},{5,9},{9,13},{2,6},{6,10},{10,14},{3,7},{... | collective-permute-start | bytes 2312 | tf_op jit(solution)/shard_map/ppermute | solution.py:19
  7.0 2.5 %copy.68 = bf16[128,32,128]{0,1,2:T(8,128)(2,1)S(1)} copy(bf16[128,32,128]{2,1,0:T(8,128)(2,1)} %param.5) | data formatting | bytes 2097152 | tf_op args[0]
  9.6 1.6 collective-permute-done.5
  13.9 4.1 %collective-permute-start = (bf16[128,1,128]{0,1,2:T(2,128)(2,1)S(1)}, bf16[128,1,128]{0,1,2:T(2,128)(2,1)}, u32[]{:S(2)}, u32[]{:S(2)}) collective-permute-start(bf16[128,1,128]{0,1,2:T(2,128)(2,1)S(1)} %get-tuple-element.47), channel_id=1, source_target_pairs={{0,4},{4,8},{8,12},{1,5},{5,9},{9,13},{2,6},{6,10},{10,14},{3,7},{... | collective-permute-start | bytes 98312 | tf_op jit(solution)/shard_map/ppermute | solution.py:19
  19.7 4.5 %collective-permute-done.1 = bf16[128,1,128]{0,1,2:T(2,128)(2,1)} collective-permute-done((bf16[128,1,128]{0,1,2:T(2,128)(2,1)S(1)}, bf16[128,1,128]{0,1,2:T(2,128)(2,1)}, u32[]{:S(2)}, u32[]{:S(2)}) %collective-permute-start.1) | collective-permute-done | bytes 32800 | tf_op jit(solution)/shard_map/ppermute | solution.py:21
  24.2 1.6 pad_maximum_fusion
  26.8 3.9 %collective-permute-start.2 = (bf16[128,34,1]{0,1,2:T(8,128)(2,1)}, bf16[128,34,1]{0,1,2:T(8,128)(2,1)}, u32[]{:S(2)}, u32[]{:S(2)}) collective-permute-start(bf16[128,34,1]{0,1,2:T(8,128)(2,1)} %get-tuple-element.37), channel_id=1, source_target_pairs={{0,1},{1,2},{2,3},{4,5},{5,6},{6,7},{8,9},{9,10},{10,11},{12,13},{... | collective-permute-start | bytes 26120 | tf_op jit(solution)/shard_map/ppermute | solution.py:19
  32.0 1.6 copy.73
  33.6 1.6 copy.76
  35.2 2.1 %pad_maximum_fusion.3 = (bf16[128,32,128]{2,1,0:T(8,128)(2,1)S(1)}, bf16[128,32,128]{2,1,0:T(8,128)(2,1)S(1)}) fusion(bf16[128,32,128]{2,1,0:T(8,128)(2,1)S(1)} %copy-done.1, bf16[128,1,128]{2,1,0:T(2,128)(2,1)} %copy.73, bf16[128,1,128]{2,1,0:T(2,128)(2,1)} %copy.76), kind=kLoop, calls=%fused_computation.30 | loop fusion | flops 4194304 | bytes 3211264 | tf_op jit(solution)/shard_map/concatenate | solution.py:17
  46.4 12.0 %all_to_all.15 = f32[14,32,128]{2,0,1:T(8,128)S(1)} all-to-all(f32[14,32,128]{2,0,1:T(8,128)S(1)} %copy.77), channel_id=1, replica_groups=mesh['groups'=2,'rows'=4,'cols'=2,'sub'=2] {'cols','sub'}, dimensions={1} | all-to-all | bytes 458752 | tf_op jit(solution)/shard_map/all_to_all | solution.py:130
  61.3 3.5 %collective-permute-start.8 = (f32[3,1,512]{2,1,0:T(1,128)S(1)}, f32[3,1,512]{2,1,0:T(1,128)S(1)}, u32[]{:S(2)}, u32[]{:S(2)}) collective-permute-start(f32[3,1,512]{2,1,0:T(1,128)S(1)} %get-tuple-element.71), channel_id=1, source_target_pairs={{0,1},{1,2},{2,3},{3,4},{4,5},{5,6},{6,7},{7,8},{8,9},{9,10},{10,1... | collective-permute-start | bytes 18440 | tf_op jit(solution)/shard_map/ppermute | solution.py:19
  66.4 2.8 %collective-permute-done.9 = f32[3,1,512]{2,1,0:T(1,128)S(1)} collective-permute-done((f32[3,1,512]{2,1,0:T(1,128)S(1)}, f32[3,1,512]{2,1,0:T(1,128)S(1)}, u32[]{:S(2)}, u32[]{:S(2)}) %collective-permute-start.9) | collective-permute-done | bytes 6176 | tf_op jit(solution)/shard_map/ppermute | solution.py:21
  69.5 4.3 %collective-permute-start.12 = (f32[4,1,512]{2,1,0:T(1,128)S(1)}, f32[4,1,512]{2,1,0:T(1,128)S(1)}, u32[]{:S(2)}, u32[]{:S(2)}) collective-permute-start(f32[4,1,512]{2,1,0:T(1,128)S(1)} %get-tuple-element.69), channel_id=1, source_target_pairs={{0,1},{1,2},{2,3},{3,4},{4,5},{5,6},{6,7},{7,8},{8,9},{9,10},{10,1... | collective-permute-start | bytes 24584 | tf_op jit(solution)/shard_map/ppermute | solution.py:19
  75.1 2.0 %collective-permute-done.13 = f32[4,1,512]{2,1,0:T(1,128)S(1)} collective-permute-done((f32[4,1,512]{2,1,0:T(1,128)S(1)}, f32[4,1,512]{2,1,0:T(1,128)S(1)}, u32[]{:S(2)}, u32[]{:S(2)}) %collective-permute-start.13) | collective-permute-done | bytes 8224 | tf_op jit(solution)/shard_map/ppermute | solution.py:21
  77.4 5.9 %collective-permute-start.14 = (f32[1,1,512]{2,1,0:T(1,128)S(1)}, f32[1,1,512]{2,1,0:T(1,128)S(1)}, u32[]{:S(2)}, u32[]{:S(2)}) collective-permute-start(f32[1,1,512]{2,1,0:T(1,128)S(1)} %get-tuple-element.87), channel_id=1, source_target_pairs={{0,1},{1,2},{2,3},{3,4},{4,5},{5,6},{6,7},{7,8},{8,9},{9,10},{10,1... | collective-permute-start | bytes 6152 | tf_op jit(solution)/shard_map/ppermute | solution.py:19
  84.6 1.7 collective-permute-done.15
  86.9 4.7 %collective-permute-start.16 = (f32[4,1,512]{2,1,0:T(1,128)S(1)}, f32[4,1,512]{2,1,0:T(1,128)S(1)}, u32[]{:S(2)}, u32[]{:S(2)}) collective-permute-start(f32[4,1,512]{2,1,0:T(1,128)S(1)} %get-tuple-element.67), channel_id=1, source_target_pairs={{0,1},{1,2},{2,3},{3,4},{4,5},{5,6},{6,7},{7,8},{8,9},{9,10},{10,1... | collective-permute-start | bytes 24584 | tf_op jit(solution)/shard_map/ppermute | solution.py:19
  92.9 1.8 collective-permute-done.17
  95.6 33.0 %all-reduce.8 = (f32[]{:T(128)}, f32[]{:T(128)}) all-reduce(f32[]{:T(128)} %get-tuple-element.8, f32[]{:T(128)} %get-tuple-element.7), channel_id=1, replica_groups=mesh['groups'=2,'rows'=4,'cols'=2,'sub'=2] {'rows','cols','sub'}, use_global_device_ids=true, to_apply=%region_1.2 | all-reduce | flops 2 | bytes 16 | tf_op jit(solution)/shard_map/psum | solution.py:116
  132.5 1.7 collective-permute-done.19
  134.8 2.1 %collective-permute-start.20 = (f32[4,1,512]{2,1,0:T(1,128)S(1)}, f32[4,1,512]{2,1,0:T(1,128)S(1)}, u32[]{:S(2)}, u32[]{:S(2)}) collective-permute-start(f32[4,1,512]{2,1,0:T(1,128)S(1)} %get-tuple-element.65), channel_id=1, source_target_pairs={{0,1},{1,2},{2,3},{3,4},{4,5},{5,6},{6,7},{7,8},{8,9},{9,10},{10,1... | collective-permute-start | bytes 24584 | tf_op jit(solution)/shard_map/ppermute | solution.py:19
  138.2 1.8 collective-permute-done.21
  140.9 32.0 %all-reduce.7 = (f32[]{:T(128)}, f32[]{:T(128)}) all-reduce(f32[]{:T(128)} %get-tuple-element.6, f32[]{:T(128)} %get-tuple-element.5), channel_id=1, replica_groups=mesh['groups'=2,'rows'=4,'cols'=2,'sub'=2] {'rows','cols','sub'}, use_global_device_ids=true, to_apply=%region_5.6 | all-reduce | flops 2 | bytes 16 | tf_op jit(solution)/shard_map/psum | solution.py:116
  (129 shorter events, 33.8 us)
Async XLA Ops:
  0.0 45.1 %copy-start = (f32[2,64]{1,0:T(2,128)S(1)}, f32[2,64]{1,0:T(2,128)}, u32[]{:S(2)}) copy-start(f32[2,64]{1,0:T(2,128)} %param.8) | copy-start | bytes 1540
  0.8 8.8 %collective-permute-start.4 = (bf16[3,1,128]{2,1,0:T(2,128)(2,1)S(1)}, bf16[3,1,128]{2,1,0:T(2,128)(2,1)S(1)}, u32[]{:S(2)}, u32[]{:S(2)}) collective-permute-start(bf16[3,1,128]{2,1,0:T(2,128)(2,1)S(1)} %get-tuple-element.77), channel_id=1, source_target_pairs={{0,4},{4,8},{8,12},{1,5},{5,9},{9,13},{2,6},{6,10},{10,14},{3,7},{... | collective-permute-start | bytes 2312 | tf_op jit(solution)/shard_map/ppermute | solution.py:19
  5.7 5.5 %collective-permute-start.5 = (bf16[3,1,128]{2,1,0:T(2,128)(2,1)S(1)}, bf16[3,1,128]{2,1,0:T(2,128)(2,1)S(1)}, u32[]{:S(2)}, u32[]{:S(2)}) collective-permute-start(bf16[3,1,128]{2,1,0:T(2,128)(2,1)S(1)} %get-tuple-element.78), channel_id=1, source_target_pairs={{4,0},{8,4},{12,8},{5,1},{9,5},{13,9},{6,2},{10,6},{14,10},{7,3},{... | collective-permute-start | bytes 2312 | tf_op jit(solution)/shard_map/ppermute | solution.py:21
  11.3 8.0 %collective-permute-start.6 = (bf16[3,34,1]{2,1,0:T(8,128)(2,1)S(1)}, bf16[3,34,1]{2,1,0:T(8,128)(2,1)S(1)}, u32[]{:S(2)}, u32[]{:S(2)}) collective-permute-start(bf16[3,34,1]{2,1,0:T(8,128)(2,1)S(1)} %get-tuple-element.75), channel_id=1, source_target_pairs={{0,1},{1,2},{2,3},{4,5},{5,6},{6,7},{8,9},{9,10},{10,11},{12,13},{... | collective-permute-start | bytes 620 | tf_op jit(solution)/shard_map/ppermute | solution.py:19
  12.6 6.7 %collective-permute-start.7 = (bf16[3,34,1]{2,1,0:T(8,128)(2,1)S(1)}, bf16[3,34,1]{2,1,0:T(8,128)(2,1)S(1)}, u32[]{:S(2)}, u32[]{:S(2)}) collective-permute-start(bf16[3,34,1]{2,1,0:T(8,128)(2,1)S(1)} %get-tuple-element.76), channel_id=1, source_target_pairs={{1,0},{2,1},{3,2},{5,4},{6,5},{7,6},{9,8},{10,9},{11,10},{13,12},{... | collective-permute-start | bytes 620 | tf_op jit(solution)/shard_map/ppermute | solution.py:21
  13.9 5.8 %collective-permute-start = (bf16[128,1,128]{0,1,2:T(2,128)(2,1)S(1)}, bf16[128,1,128]{0,1,2:T(2,128)(2,1)}, u32[]{:S(2)}, u32[]{:S(2)}) collective-permute-start(bf16[128,1,128]{0,1,2:T(2,128)(2,1)S(1)} %get-tuple-element.47), channel_id=1, source_target_pairs={{0,4},{4,8},{8,12},{1,5},{5,9},{9,13},{2,6},{6,10},{10,14},{3,7},{... | collective-permute-start | bytes 98312 | tf_op jit(solution)/shard_map/ppermute | solution.py:19
  18.0 6.3 %collective-permute-start.1 = (bf16[128,1,128]{0,1,2:T(2,128)(2,1)S(1)}, bf16[128,1,128]{0,1,2:T(2,128)(2,1)}, u32[]{:S(2)}, u32[]{:S(2)}) collective-permute-start(bf16[128,1,128]{0,1,2:T(2,128)(2,1)S(1)} %get-tuple-element.48), channel_id=1, source_target_pairs={{4,0},{8,4},{12,8},{5,1},{9,5},{13,9},{6,2},{10,6},{14,10},{7,3},{... | collective-permute-start | bytes 98312 | tf_op jit(solution)/shard_map/ppermute | solution.py:21
  26.8 11.0 %collective-permute-start.2 = (bf16[128,34,1]{0,1,2:T(8,128)(2,1)}, bf16[128,34,1]{0,1,2:T(8,128)(2,1)}, u32[]{:S(2)}, u32[]{:S(2)}) collective-permute-start(bf16[128,34,1]{0,1,2:T(8,128)(2,1)} %get-tuple-element.37), channel_id=1, source_target_pairs={{0,1},{1,2},{2,3},{4,5},{5,6},{6,7},{8,9},{9,10},{10,11},{12,13},{... | collective-permute-start | bytes 26120 | tf_op jit(solution)/shard_map/ppermute | solution.py:19
  30.7 9.2 %collective-permute-start.3 = (bf16[128,34,1]{0,1,2:T(8,128)(2,1)}, bf16[128,34,1]{0,1,2:T(8,128)(2,1)}, u32[]{:S(2)}, u32[]{:S(2)}) collective-permute-start(bf16[128,34,1]{0,1,2:T(8,128)(2,1)} %get-tuple-element.38), channel_id=1, source_target_pairs={{1,0},{2,1},{3,2},{5,4},{6,5},{7,6},{9,8},{10,9},{11,10},{13,12},{... | collective-permute-start | bytes 26120 | tf_op jit(solution)/shard_map/ppermute | solution.py:21
  58.5 18.8 %copy-start.5 = (s32[8,512]{1,0:T(8,128)S(1)}, s32[8,512]{1,0:T(8,128)}, u32[]{:S(2)}) copy-start(s32[8,512]{1,0:T(8,128)} %param.9) | copy-start | bytes 49156
  58.6 7.6 %collective-permute-start.10 = (f32[1,1,512]{2,1,0:T(1,128)S(1)}, f32[1,1,512]{2,1,0:T(1,128)S(1)}, u32[]{:S(2)}, u32[]{:S(2)}) collective-permute-start(f32[1,1,512]{2,1,0:T(1,128)S(1)} %get-tuple-element.89), channel_id=1, source_target_pairs={{0,1},{1,2},{2,3},{3,4},{4,5},{5,6},{6,7},{7,8},{8,9},{9,10},{10,1... | collective-permute-start | bytes 6152 | tf_op jit(solution)/shard_map/ppermute | solution.py:19
  60.0 6.2 %collective-permute-start.11 = (f32[1,1,512]{2,1,0:T(1,128)S(1)}, f32[1,1,512]{2,1,0:T(1,128)S(1)}, u32[]{:S(2)}, u32[]{:S(2)}) collective-permute-start(f32[1,1,512]{2,1,0:T(1,128)S(1)} %get-tuple-element.90), channel_id=1, source_target_pairs={{1,0},{2,1},{3,2},{4,3},{5,4},{6,5},{7,6},{8,7},{9,8},{10,9},{11,1... | collective-permute-start | bytes 6152 | tf_op jit(solution)/shard_map/ppermute | solution.py:21
  61.3 5.1 %collective-permute-start.8 = (f32[3,1,512]{2,1,0:T(1,128)S(1)}, f32[3,1,512]{2,1,0:T(1,128)S(1)}, u32[]{:S(2)}, u32[]{:S(2)}) collective-permute-start(f32[3,1,512]{2,1,0:T(1,128)S(1)} %get-tuple-element.71), channel_id=1, source_target_pairs={{0,1},{1,2},{2,3},{3,4},{4,5},{5,6},{6,7},{7,8},{8,9},{9,10},{10,1... | collective-permute-start | bytes 18440 | tf_op jit(solution)/shard_map/ppermute | solution.py:19
  64.8 4.3 %collective-permute-start.9 = (f32[3,1,512]{2,1,0:T(1,128)S(1)}, f32[3,1,512]{2,1,0:T(1,128)S(1)}, u32[]{:S(2)}, u32[]{:S(2)}) collective-permute-start(f32[3,1,512]{2,1,0:T(1,128)S(1)} %get-tuple-element.72), channel_id=1, source_target_pairs={{1,0},{2,1},{3,2},{4,3},{5,4},{6,5},{7,6},{8,7},{9,8},{10,9},{11,1... | collective-permute-start | bytes 18440 | tf_op jit(solution)/shard_map/ppermute | solution.py:21
  69.5 5.6 %collective-permute-start.12 = (f32[4,1,512]{2,1,0:T(1,128)S(1)}, f32[4,1,512]{2,1,0:T(1,128)S(1)}, u32[]{:S(2)}, u32[]{:S(2)}) collective-permute-start(f32[4,1,512]{2,1,0:T(1,128)S(1)} %get-tuple-element.69), channel_id=1, source_target_pairs={{0,1},{1,2},{2,3},{3,4},{4,5},{5,6},{6,7},{7,8},{8,9},{9,10},{10,1... | collective-permute-start | bytes 24584 | tf_op jit(solution)/shard_map/ppermute | solution.py:19
  73.8 3.3 %collective-permute-start.13 = (f32[4,1,512]{2,1,0:T(1,128)S(1)}, f32[4,1,512]{2,1,0:T(1,128)S(1)}, u32[]{:S(2)}, u32[]{:S(2)}) collective-permute-start(f32[4,1,512]{2,1,0:T(1,128)S(1)} %get-tuple-element.70), channel_id=1, source_target_pairs={{1,0},{2,1},{3,2},{4,3},{5,4},{6,5},{7,6},{8,7},{9,8},{10,9},{11,1... | collective-permute-start | bytes 24584 | tf_op jit(solution)/shard_map/ppermute | solution.py:21
  77.4 7.2 %collective-permute-start.14 = (f32[1,1,512]{2,1,0:T(1,128)S(1)}, f32[1,1,512]{2,1,0:T(1,128)S(1)}, u32[]{:S(2)}, u32[]{:S(2)}) collective-permute-start(f32[1,1,512]{2,1,0:T(1,128)S(1)} %get-tuple-element.87), channel_id=1, source_target_pairs={{0,1},{1,2},{2,3},{3,4},{4,5},{5,6},{6,7},{7,8},{8,9},{9,10},{10,1... | collective-permute-start | bytes 6152 | tf_op jit(solution)/shard_map/ppermute | solution.py:19
  83.3 3.1 %collective-permute-start.15 = (f32[1,1,512]{2,1,0:T(1,128)S(1)}, f32[1,1,512]{2,1,0:T(1,128)S(1)}, u32[]{:S(2)}, u32[]{:S(2)}) collective-permute-start(f32[1,1,512]{2,1,0:T(1,128)S(1)} %get-tuple-element.88), channel_id=1, source_target_pairs={{1,0},{2,1},{3,2},{4,3},{5,4},{6,5},{7,6},{8,7},{9,8},{10,9},{11,1... | collective-permute-start | bytes 6152 | tf_op jit(solution)/shard_map/ppermute | solution.py:21
  86.9 6.0 %collective-permute-start.16 = (f32[4,1,512]{2,1,0:T(1,128)S(1)}, f32[4,1,512]{2,1,0:T(1,128)S(1)}, u32[]{:S(2)}, u32[]{:S(2)}) collective-permute-start(f32[4,1,512]{2,1,0:T(1,128)S(1)} %get-tuple-element.67), channel_id=1, source_target_pairs={{0,1},{1,2},{2,3},{3,4},{4,5},{5,6},{6,7},{7,8},{8,9},{9,10},{10,1... | collective-permute-start | bytes 24584 | tf_op jit(solution)/shard_map/ppermute | solution.py:19
  91.6 3.1 %collective-permute-start.17 = (f32[4,1,512]{2,1,0:T(1,128)S(1)}, f32[4,1,512]{2,1,0:T(1,128)S(1)}, u32[]{:S(2)}, u32[]{:S(2)}) collective-permute-start(f32[4,1,512]{2,1,0:T(1,128)S(1)} %get-tuple-element.68), channel_id=1, source_target_pairs={{1,0},{2,1},{3,2},{4,3},{5,4},{6,5},{7,6},{8,7},{9,8},{10,9},{11,1... | collective-permute-start | bytes 24584 | tf_op jit(solution)/shard_map/ppermute | solution.py:21
  129.9 2.6 %collective-permute-start.18 = (f32[1,1,512]{2,1,0:T(1,128)S(1)}, f32[1,1,512]{2,1,0:T(1,128)S(1)}, u32[]{:S(2)}, u32[]{:S(2)}) collective-permute-start(f32[1,1,512]{2,1,0:T(1,128)S(1)} %get-tuple-element.85), channel_id=1, source_target_pairs={{0,1},{1,2},{2,3},{3,4},{4,5},{5,6},{6,7},{7,8},{8,9},{9,10},{10,1... | collective-permute-start | bytes 6152 | tf_op jit(solution)/shard_map/ppermute | solution.py:19
  131.2 3.1 %collective-permute-start.19 = (f32[1,1,512]{2,1,0:T(1,128)S(1)}, f32[1,1,512]{2,1,0:T(1,128)S(1)}, u32[]{:S(2)}, u32[]{:S(2)}) collective-permute-start(f32[1,1,512]{2,1,0:T(1,128)S(1)} %get-tuple-element.86), channel_id=1, source_target_pairs={{1,0},{2,1},{3,2},{4,3},{5,4},{6,5},{7,6},{8,7},{9,8},{10,9},{11,1... | collective-permute-start | bytes 6152 | tf_op jit(solution)/shard_map/ppermute | solution.py:21
  134.8 3.4 %collective-permute-start.20 = (f32[4,1,512]{2,1,0:T(1,128)S(1)}, f32[4,1,512]{2,1,0:T(1,128)S(1)}, u32[]{:S(2)}, u32[]{:S(2)}) collective-permute-start(f32[4,1,512]{2,1,0:T(1,128)S(1)} %get-tuple-element.65), channel_id=1, source_target_pairs={{0,1},{1,2},{2,3},{3,4},{4,5},{5,6},{6,7},{7,8},{8,9},{9,10},{10,1... | collective-permute-start | bytes 24584 | tf_op jit(solution)/shard_map/ppermute | solution.py:19
  136.9 3.1 %collective-permute-start.21 = (f32[4,1,512]{2,1,0:T(1,128)S(1)}, f32[4,1,512]{2,1,0:T(1,128)S(1)}, u32[]{:S(2)}, u32[]{:S(2)}) collective-permute-start(f32[4,1,512]{2,1,0:T(1,128)S(1)} %get-tuple-element.66), channel_id=1, source_target_pairs={{1,0},{2,1},{3,2},{4,3},{5,4},{6,5},{7,6},{8,7},{9,8},{10,9},{11,1... | collective-permute-start | bytes 24584 | tf_op jit(solution)/shard_map/ppermute | solution.py:21
  (4 other events, 24.3 us)
where the time goes:
time: 179 us; the launch traced here: 178 us
  blocking collectives  77 us (43%)
  starting transfers between devices  51.5 us (29%)
  waiting for transfers between devices  17.9 us (10%)
  local copies, waits for them, and re-layouts  10.2 us (6%)
  other arithmetic  9.49 us (5%)
  between operations  6.62 us (4%)
  matrix products  5.29 us (3%)
    psum x2, blocking collectives, global_sums(): return lax.psum((values[0], values[1]), ('rows', 'cols', 'sub'))  65 us
    ppermute x11, starting transfers between devices, with_halo(): lax.ppermute(tail, axis, [(i, (i + 1) % count) for i in range(ends)])  37.3 us
    ppermute x11, waiting for transfers between devices, with_halo(): lax.ppermute(head, axis, [((i + 1) % count, i) for i in range(ends)])  17.8 us
    ppermute x11, starting transfers between devices, with_halo(): lax.ppermute(head, axis, [((i + 1) % count, i) for i in range(ends)])  14.2 us
    all_to_all x1, blocking collectives, on_device(): lax.all_to_all(stacked, ('cols', 'sub'), split_axis=1, concat_axis=2, til...  12 us
    concatenate x7, other arithmetic, with_halo(): jnp.concatenate([lax.ppermute(tail, axis, [(i, (i + 1) % count) for i in...  5.03 us
    dot_general x9, matrix products, head_maps(): jnp.dot(conv_weight[shift_r, shift_c], window_cell_count, preferred_eleme...  4.64 us
  transfers between devices with their start and end apart: 22, of which 8 were waited for; matrix products, arithmetic and copies ran while one was open for 6% of the time, Pallas kernels for 0%

commit v1 on v0

--- a/solution.py
+++ b/solution.py
@@ -113,7 +113,7 @@
 
 
 def global_sums(values):
-    return lax.psum((values[0], values[1]), ("rows", "cols", "sub"))
+    return lax.psum(lax.psum((values[0], values[1]), ("cols", "sub")), "rows")
 
 
 def on_device(features, guide_image, conv_weight, head_weight, pixel_mask):

time: 179 us -> 159 us (0.89)
  blocking collectives: 77 us -> 54.1 us
  starting transfers between devices: 51.5 us -> 53.7 us
    psum x2 -> x4, blocking collectives: 65 us -> 42.1 us  [global_sums(): return lax.psum(lax.psum((values[0], values[1]), ('cols', 'sub')), 'rows')]
    ppermute x11, starting transfers between devices: 37.3 us -> 39.5 us  [with_halo(): lax.ppermute(tail, axis, [(i, (i + 1) % count) for i in range(ends)])]
  transfers between devices with their start and end apart: 22 -> 22, of which waited for: 8 -> 8; matrix products, arithmetic and copies ran while one was open for 6% -> 7% of each run, Pallas kernels for 0% -> 0%
where the time goes in v1:
time: 159 us; the launch traced here: 158 us
  blocking collectives  54.1 us (34%)
  starting transfers between devices  53.7 us (34%)
  waiting for transfers between devices  18.5 us (12%)
  local copies, waits for them, and re-layouts  10.2 us (6%)
  other arithmetic  9.55 us (6%)
  between operations  6.78 us (4%)
  matrix products  5.29 us (3%)
    psum x4, blocking collectives, global_sums(): return lax.psum(lax.psum((values[0], values[1]), ('cols', 'sub')), 'rows')  42.1 us
    ppermute x11, starting transfers between devices, with_halo(): lax.ppermute(tail, axis, [(i, (i + 1) % count) for i in range(ends)])  39.5 us
    ppermute x11, waiting for transfers between devices, with_halo(): lax.ppermute(head, axis, [((i + 1) % count, i) for i in range(ends)])  18.5 us
    ppermute x11, starting transfers between devices, with_halo(): lax.ppermute(head, axis, [((i + 1) % count, i) for i in range(ends)])  14.2 us
    all_to_all x1, blocking collectives, on_device(): lax.all_to_all(stacked, ('cols', 'sub'), split_axis=1, concat_axis=2, til...  11.9 us
    concatenate x7, other arithmetic, with_halo(): jnp.concatenate([lax.ppermute(tail, axis, [(i, (i + 1) % count) for i in...  5.03 us
    dot_general x9, matrix products, head_maps(): jnp.dot(conv_weight[shift_r, shift_c], window_cell_count, preferred_eleme...  4.64 us
  transfers between devices with their start and end apart: 22, of which 8 were waited for; matrix products, arithmetic and copies ran while one was open for 7% of the time, Pallas kernels for 0%

profile of v1, /device:TPU:0, one launch (start us, length us, event | category | flops | bytes accessed | tf_op | source)
XLA Modules:
  0.0 158.2 jit_solution(14834688065611317212)
XLA Ops:
  0.8 4.9 %collective-permute-start.4 = (bf16[3,1,128]{2,1,0:T(2,128)(2,1)S(1)}, bf16[3,1,128]{2,1,0:T(2,128)(2,1)S(1)}, u32[]{:S(2)}, u32[]{:S(2)}) collective-permute-start(bf16[3,1,128]{2,1,0:T(2,128)(2,1)S(1)} %get-tuple-element.81), channel_id=1, source_target_pairs={{0,4},{4,8},{8,12},{1,5},{5,9},{9,13},{2,6},{6,10},{10,14},{3,7},{... | collective-permute-start | bytes 2312 | tf_op jit(solution)/shard_map/ppermute | solution.py:19
  7.0 2.5 %copy.68 = bf16[128,32,128]{0,1,2:T(8,128)(2,1)S(1)} copy(bf16[128,32,128]{2,1,0:T(8,128)(2,1)} %param.5) | data formatting | bytes 2097152 | tf_op args[0]
  13.9 4.1 %collective-permute-start = (bf16[128,1,128]{0,1,2:T(2,128)(2,1)S(1)}, bf16[128,1,128]{0,1,2:T(2,128)(2,1)}, u32[]{:S(2)}, u32[]{:S(2)}) collective-permute-start(bf16[128,1,128]{0,1,2:T(2,128)(2,1)S(1)} %get-tuple-element.51), channel_id=1, source_target_pairs={{0,4},{4,8},{8,12},{1,5},{5,9},{9,13},{2,6},{6,10},{10,14},{3,7},{... | collective-permute-start | bytes 98312 | tf_op jit(solution)/shard_map/ppermute | solution.py:19
  19.7 4.5 %collective-permute-done.1 = bf16[128,1,128]{0,1,2:T(2,128)(2,1)} collective-permute-done((bf16[128,1,128]{0,1,2:T(2,128)(2,1)S(1)}, bf16[128,1,128]{0,1,2:T(2,128)(2,1)}, u32[]{:S(2)}, u32[]{:S(2)}) %collective-permute-start.1) | collective-permute-done | bytes 32800 | tf_op jit(solution)/shard_map/ppermute | solution.py:21
  24.2 1.6 %pad_maximum_fusion = bf16[128,34,128]{0,1,2:T(8,128)(2,1)S(1)} fusion(bf16[128,1,128]{0,1,2:T(2,128)(2,1)} %collective-permute-done.1, bf16[128,32,128]{0,1,2:T(8,128)(2,1)S(1)} %copy.68, bf16[128,1,128]{0,1,2:T(2,128)(2,1)} %collective-permute-done), kind=kLoop, calls=%fused_computation.17 | loop fusion | flops 3342336 | bytes 2228224 | tf_op jit(solution)/shard_map/concatenate | solution.py:17
  26.8 3.9 %collective-permute-start.2 = (bf16[128,34,1]{0,1,2:T(8,128)(2,1)}, bf16[128,34,1]{0,1,2:T(8,128)(2,1)}, u32[]{:S(2)}, u32[]{:S(2)}) collective-permute-start(bf16[128,34,1]{0,1,2:T(8,128)(2,1)} %get-tuple-element.41), channel_id=1, source_target_pairs={{0,1},{1,2},{2,3},{4,5},{5,6},{6,7},{8,9},{9,10},{10,11},{12,13},{... | collective-permute-start | bytes 26120 | tf_op jit(solution)/shard_map/ppermute | solution.py:19
  32.0 1.6 %copy.73 = bf16[128,1,128]{2,1,0:T(2,128)(2,1)} copy(bf16[128,1,128]{0,1,2:T(2,128)(2,1)} %collective-permute-done) | data formatting | bytes 65536 | tf_op jit(solution)/shard_map/ppermute | solution.py:19
  35.2 2.1 %pad_maximum_fusion.3 = (bf16[128,32,128]{2,1,0:T(8,128)(2,1)S(1)}, bf16[128,32,128]{2,1,0:T(8,128)(2,1)S(1)}) fusion(bf16[128,32,128]{2,1,0:T(8,128)(2,1)S(1)} %copy-done.1, bf16[128,1,128]{2,1,0:T(2,128)(2,1)} %copy.73, bf16[128,1,128]{2,1,0:T(2,128)(2,1)} %copy.76), kind=kLoop, calls=%fused_computation.30 | loop fusion | flops 4194304 | bytes 3211264 | tf_op jit(solution)/shard_map/concatenate | solution.py:17
  46.3 11.9 %all_to_all.15 = f32[14,32,128]{2,0,1:T(8,128)S(1)} all-to-all(f32[14,32,128]{2,0,1:T(8,128)S(1)} %copy.77), channel_id=1, replica_groups=mesh['groups'=2,'rows'=4,'cols'=2,'sub'=2] {'cols','sub'}, dimensions={1} | all-to-all | bytes 458752 | tf_op jit(solution)/shard_map/all_to_all | solution.py:130
  61.3 3.5 %collective-permute-start.8 = (f32[3,1,512]{2,1,0:T(1,128)S(1)}, f32[3,1,512]{2,1,0:T(1,128)S(1)}, u32[]{:S(2)}, u32[]{:S(2)}) collective-permute-start(f32[3,1,512]{2,1,0:T(1,128)S(1)} %get-tuple-element.75), channel_id=1, source_target_pairs={{0,1},{1,2},{2,3},{3,4},{4,5},{5,6},{6,7},{7,8},{8,9},{9,10},{10,1... | collective-permute-start | bytes 18440 | tf_op jit(solution)/shard_map/ppermute | solution.py:19
  66.3 2.8 %collective-permute-done.9 = f32[3,1,512]{2,1,0:T(1,128)S(1)} collective-permute-done((f32[3,1,512]{2,1,0:T(1,128)S(1)}, f32[3,1,512]{2,1,0:T(1,128)S(1)}, u32[]{:S(2)}, u32[]{:S(2)}) %collective-permute-start.9) | collective-permute-done | bytes 6176 | tf_op jit(solution)/shard_map/ppermute | solution.py:21
  69.5 4.3 %collective-permute-start.12 = (f32[4,1,512]{2,1,0:T(1,128)S(1)}, f32[4,1,512]{2,1,0:T(1,128)S(1)}, u32[]{:S(2)}, u32[]{:S(2)}) collective-permute-start(f32[4,1,512]{2,1,0:T(1,128)S(1)} %get-tuple-element.73), channel_id=1, source_target_pairs={{0,1},{1,2},{2,3},{3,4},{4,5},{5,6},{6,7},{7,8},{8,9},{9,10},{10,1... | collective-permute-start | bytes 24584 | tf_op jit(solution)/shard_map/ppermute | solution.py:19
  75.1 2.0 %collective-permute-done.13 = f32[4,1,512]{2,1,0:T(1,128)S(1)} collective-permute-done((f32[4,1,512]{2,1,0:T(1,128)S(1)}, f32[4,1,512]{2,1,0:T(1,128)S(1)}, u32[]{:S(2)}, u32[]{:S(2)}) %collective-permute-start.13) | collective-permute-done | bytes 8224 | tf_op jit(solution)/shard_map/ppermute | solution.py:21
  77.4 5.9 %collective-permute-start.14 = (f32[1,1,512]{2,1,0:T(1,128)S(1)}, f32[1,1,512]{2,1,0:T(1,128)S(1)}, u32[]{:S(2)}, u32[]{:S(2)}) collective-permute-start(f32[1,1,512]{2,1,0:T(1,128)S(1)} %get-tuple-element.91), channel_id=1, source_target_pairs={{0,1},{1,2},{2,3},{3,4},{4,5},{5,6},{6,7},{7,8},{8,9},{9,10},{10,1... | collective-permute-start | bytes 6152 | tf_op jit(solution)/shard_map/ppermute | solution.py:19
  84.6 1.7 %collective-permute-done.15 = f32[1,1,512]{2,1,0:T(1,128)S(1)} collective-permute-done((f32[1,1,512]{2,1,0:T(1,128)S(1)}, f32[1,1,512]{2,1,0:T(1,128)S(1)}, u32[]{:S(2)}, u32[]{:S(2)}) %collective-permute-start.15) | collective-permute-done | bytes 2080 | tf_op jit(solution)/shard_map/ppermute | solution.py:21
  86.9 4.7 %collective-permute-start.16 = (f32[4,1,512]{2,1,0:T(1,128)S(1)}, f32[4,1,512]{2,1,0:T(1,128)S(1)}, u32[]{:S(2)}, u32[]{:S(2)}) collective-permute-start(f32[4,1,512]{2,1,0:T(1,128)S(1)} %get-tuple-element.71), channel_id=1, source_target_pairs={{0,1},{1,2},{2,3},{3,4},{4,5},{5,6},{6,7},{7,8},{8,9},{9,10},{10,1... | collective-permute-start | bytes 24584 | tf_op jit(solution)/shard_map/ppermute | solution.py:19
  92.9 1.8 %collective-permute-done.17 = f32[4,1,512]{2,1,0:T(1,128)S(1)} collective-permute-done((f32[4,1,512]{2,1,0:T(1,128)S(1)}, f32[4,1,512]{2,1,0:T(1,128)S(1)}, u32[]{:S(2)}, u32[]{:S(2)}) %collective-permute-start.17) | collective-permute-done | bytes 8224 | tf_op jit(solution)/shard_map/ppermute | solution.py:21
  95.6 11.3 %all-reduce.8 = (f32[]{:T(128)}, f32[]{:T(128)}) all-reduce(f32[]{:T(128)} %get-tuple-element.8, f32[]{:T(128)} %get-tuple-element.7), channel_id=1, replica_groups=mesh['groups'=2,'rows'=4,'cols'=2,'sub'=2] {'cols','sub'}, use_global_device_ids=true, to_apply=%region_1.2 | all-reduce | flops 2 | bytes 16 | tf_op jit(solution)/shard_map/psum | solution.py:116
  106.9 10.1 %all-reduce.10 = (f32[]{:T(128)}, f32[]{:T(128)}) all-reduce(f32[]{:T(128)} %get-tuple-element.11, f32[]{:T(128)} %get-tuple-element.12), channel_id=1, replica_groups=mesh['groups'=2,'rows'=4,'cols'=2,'sub'=2] {'rows'}, use_global_device_ids=true, to_apply=%region_2.3 | all-reduce | flops 2 | bytes 16 | tf_op jit(solution)/shard_map/psum | solution.py:116
  121.1 2.4 %collective-permute-done.19 = f32[1,1,512]{2,1,0:T(1,128)S(1)} collective-permute-done((f32[1,1,512]{2,1,0:T(1,128)S(1)}, f32[1,1,512]{2,1,0:T(1,128)S(1)}, u32[]{:S(2)}, u32[]{:S(2)}) %collective-permute-start.19) | collective-permute-done | bytes 2080 | tf_op jit(solution)/shard_map/ppermute | solution.py:21
  124.0 4.3 %collective-permute-start.20 = (f32[4,1,512]{2,1,0:T(1,128)S(1)}, f32[4,1,512]{2,1,0:T(1,128)S(1)}, u32[]{:S(2)}, u32[]{:S(2)}) collective-permute-start(f32[4,1,512]{2,1,0:T(1,128)S(1)} %get-tuple-element.69), channel_id=1, source_target_pairs={{0,1},{1,2},{2,3},{3,4},{4,5},{5,6},{6,7},{7,8},{8,9},{9,10},{10,1... | collective-permute-start | bytes 24584 | tf_op jit(solution)/shard_map/ppermute | solution.py:19
  129.6 1.8 %collective-permute-done.21 = f32[4,1,512]{2,1,0:T(1,128)S(1)} collective-permute-done((f32[4,1,512]{2,1,0:T(1,128)S(1)}, f32[4,1,512]{2,1,0:T(1,128)S(1)}, u32[]{:S(2)}, u32[]{:S(2)}) %collective-permute-start.21) | collective-permute-done | bytes 8224 | tf_op jit(solution)/shard_map/ppermute | solution.py:21
  132.3 11.6 %all-reduce.7 = (f32[]{:T(128)}, f32[]{:T(128)}) all-reduce(f32[]{:T(128)} %get-tuple-element.6, f32[]{:T(128)} %get-tuple-element.5), channel_id=1, replica_groups=mesh['groups'=2,'rows'=4,'cols'=2,'sub'=2] {'cols','sub'}, use_global_device_ids=true, to_apply=%region_7.8 | all-reduce | flops 2 | bytes 16 | tf_op jit(solution)/shard_map/psum | solution.py:116
  143.9 9.1 %all-reduce.9 = (f32[]{:T(128)}, f32[]{:T(128)}) all-reduce(f32[]{:T(128)} %get-tuple-element.9, f32[]{:T(128)} %get-tuple-element.10), channel_id=1, replica_groups=mesh['groups'=2,'rows'=4,'cols'=2,'sub'=2] {'rows'}, use_global_device_ids=true, to_apply=%region_8.9 | all-reduce | flops 2 | bytes 16 | tf_op jit(solution)/shard_map/psum | solution.py:116
  (131 shorter events, 37.0 us)
Async XLA Ops:
  0.0 45.1 %copy-start = (f32[2,64]{1,0:T(2,128)S(1)}, f32[2,64]{1,0:T(2,128)}, u32[]{:S(2)}) copy-start(f32[2,64]{1,0:T(2,128)} %param.8) | copy-start | bytes 1540
  0.8 8.8 %collective-permute-start.4 = (bf16[3,1,128]{2,1,0:T(2,128)(2,1)S(1)}, bf16[3,1,128]{2,1,0:T(2,128)(2,1)S(1)}, u32[]{:S(2)}, u32[]{:S(2)}) collective-permute-start(bf16[3,1,128]{2,1,0:T(2,128)(2,1)S(1)} %get-tuple-element.81), channel_id=1, source_target_pairs={{0,4},{4,8},{8,12},{1,5},{5,9},{9,13},{2,6},{6,10},{10,14},{3,7},{... | collective-permute-start | bytes 2312 | tf_op jit(solution)/shard_map/ppermute | solution.py:19
  5.7 5.5 %collective-permute-start.5 = (bf16[3,1,128]{2,1,0:T(2,128)(2,1)S(1)}, bf16[3,1,128]{2,1,0:T(2,128)(2,1)S(1)}, u32[]{:S(2)}, u32[]{:S(2)}) collective-permute-start(bf16[3,1,128]{2,1,0:T(2,128)(2,1)S(1)} %get-tuple-element.82), channel_id=1, source_target_pairs={{4,0},{8,4},{12,8},{5,1},{9,5},{13,9},{6,2},{10,6},{14,10},{7,3},{... | collective-permute-start | bytes 2312 | tf_op jit(solution)/shard_map/ppermute | solution.py:21
  11.3 8.0 %collective-permute-start.6 = (bf16[3,34,1]{2,1,0:T(8,128)(2,1)S(1)}, bf16[3,34,1]{2,1,0:T(8,128)(2,1)S(1)}, u32[]{:S(2)}, u32[]{:S(2)}) collective-permute-start(bf16[3,34,1]{2,1,0:T(8,128)(2,1)S(1)} %get-tuple-element.79), channel_id=1, source_target_pairs={{0,1},{1,2},{2,3},{4,5},{5,6},{6,7},{8,9},{9,10},{10,11},{12,13},{... | collective-permute-start | bytes 620 | tf_op jit(solution)/shard_map/ppermute | solution.py:19
  12.6 6.7 %collective-permute-start.7 = (bf16[3,34,1]{2,1,0:T(8,128)(2,1)S(1)}, bf16[3,34,1]{2,1,0:T(8,128)(2,1)S(1)}, u32[]{:S(2)}, u32[]{:S(2)}) collective-permute-start(bf16[3,34,1]{2,1,0:T(8,128)(2,1)S(1)} %get-tuple-element.80), channel_id=1, source_target_pairs={{1,0},{2,1},{3,2},{5,4},{6,5},{7,6},{9,8},{10,9},{11,10},{13,12},{... | collective-permute-start | bytes 620 | tf_op jit(solution)/shard_map/ppermute | solution.py:21
  13.9 5.8 %collective-permute-start = (bf16[128,1,128]{0,1,2:T(2,128)(2,1)S(1)}, bf16[128,1,128]{0,1,2:T(2,128)(2,1)}, u32[]{:S(2)}, u32[]{:S(2)}) collective-permute-start(bf16[128,1,128]{0,1,2:T(2,128)(2,1)S(1)} %get-tuple-element.51), channel_id=1, source_target_pairs={{0,4},{4,8},{8,12},{1,5},{5,9},{9,13},{2,6},{6,10},{10,14},{3,7},{... | collective-permute-start | bytes 98312 | tf_op jit(solution)/shard_map/ppermute | solution.py:19
  18.0 6.3 %collective-permute-start.1 = (bf16[128,1,128]{0,1,2:T(2,128)(2,1)S(1)}, bf16[128,1,128]{0,1,2:T(2,128)(2,1)}, u32[]{:S(2)}, u32[]{:S(2)}) collective-permute-start(bf16[128,1,128]{0,1,2:T(2,128)(2,1)S(1)} %get-tuple-element.52), channel_id=1, source_target_pairs={{4,0},{8,4},{12,8},{5,1},{9,5},{13,9},{6,2},{10,6},{14,10},{7,3},{... | collective-permute-start | bytes 98312 | tf_op jit(solution)/shard_map/ppermute | solution.py:21
  26.8 11.0 %collective-permute-start.2 = (bf16[128,34,1]{0,1,2:T(8,128)(2,1)}, bf16[128,34,1]{0,1,2:T(8,128)(2,1)}, u32[]{:S(2)}, u32[]{:S(2)}) collective-permute-start(bf16[128,34,1]{0,1,2:T(8,128)(2,1)} %get-tuple-element.41), channel_id=1, source_target_pairs={{0,1},{1,2},{2,3},{4,5},{5,6},{6,7},{8,9},{9,10},{10,11},{12,13},{... | collective-permute-start | bytes 26120 | tf_op jit(solution)/shard_map/ppermute | solution.py:19
  30.7 9.2 %collective-permute-start.3 = (bf16[128,34,1]{0,1,2:T(8,128)(2,1)}, bf16[128,34,1]{0,1,2:T(8,128)(2,1)}, u32[]{:S(2)}, u32[]{:S(2)}) collective-permute-start(bf16[128,34,1]{0,1,2:T(8,128)(2,1)} %get-tuple-element.42), channel_id=1, source_target_pairs={{1,0},{2,1},{3,2},{5,4},{6,5},{7,6},{9,8},{10,9},{11,10},{13,12},{... | collective-permute-start | bytes 26120 | tf_op jit(solution)/shard_map/ppermute | solution.py:21
  58.5 18.9 %copy-start.5 = (s32[8,512]{1,0:T(8,128)S(1)}, s32[8,512]{1,0:T(8,128)}, u32[]{:S(2)}) copy-start(s32[8,512]{1,0:T(8,128)} %param.9) | copy-start | bytes 49156
  58.6 7.6 %collective-permute-start.10 = (f32[1,1,512]{2,1,0:T(1,128)S(1)}, f32[1,1,512]{2,1,0:T(1,128)S(1)}, u32[]{:S(2)}, u32[]{:S(2)}) collective-permute-start(f32[1,1,512]{2,1,0:T(1,128)S(1)} %get-tuple-element.93), channel_id=1, source_target_pairs={{0,1},{1,2},{2,3},{3,4},{4,5},{5,6},{6,7},{7,8},{8,9},{9,10},{10,1... | collective-permute-start | bytes 6152 | tf_op jit(solution)/shard_map/ppermute | solution.py:19
  59.9 6.2 %collective-permute-start.11 = (f32[1,1,512]{2,1,0:T(1,128)S(1)}, f32[1,1,512]{2,1,0:T(1,128)S(1)}, u32[]{:S(2)}, u32[]{:S(2)}) collective-permute-start(f32[1,1,512]{2,1,0:T(1,128)S(1)} %get-tuple-element.94), channel_id=1, source_target_pairs={{1,0},{2,1},{3,2},{4,3},{5,4},{6,5},{7,6},{8,7},{9,8},{10,9},{11,1... | collective-permute-start | bytes 6152 | tf_op jit(solution)/shard_map/ppermute | solution.py:21
  61.3 5.1 %collective-permute-start.8 = (f32[3,1,512]{2,1,0:T(1,128)S(1)}, f32[3,1,512]{2,1,0:T(1,128)S(1)}, u32[]{:S(2)}, u32[]{:S(2)}) collective-permute-start(f32[3,1,512]{2,1,0:T(1,128)S(1)} %get-tuple-element.75), channel_id=1, source_target_pairs={{0,1},{1,2},{2,3},{3,4},{4,5},{5,6},{6,7},{7,8},{8,9},{9,10},{10,1... | collective-permute-start | bytes 18440 | tf_op jit(solution)/shard_map/ppermute | solution.py:19
  64.8 4.3 %collective-permute-start.9 = (f32[3,1,512]{2,1,0:T(1,128)S(1)}, f32[3,1,512]{2,1,0:T(1,128)S(1)}, u32[]{:S(2)}, u32[]{:S(2)}) collective-permute-start(f32[3,1,512]{2,1,0:T(1,128)S(1)} %get-tuple-element.76), channel_id=1, source_target_pairs={{1,0},{2,1},{3,2},{4,3},{5,4},{6,5},{7,6},{8,7},{9,8},{10,9},{11,1... | collective-permute-start | bytes 18440 | tf_op jit(solution)/shard_map/ppermute | solution.py:21
  69.5 5.6 %collective-permute-start.12 = (f32[4,1,512]{2,1,0:T(1,128)S(1)}, f32[4,1,512]{2,1,0:T(1,128)S(1)}, u32[]{:S(2)}, u32[]{:S(2)}) collective-permute-start(f32[4,1,512]{2,1,0:T(1,128)S(1)} %get-tuple-element.73), channel_id=1, source_target_pairs={{0,1},{1,2},{2,3},{3,4},{4,5},{5,6},{6,7},{7,8},{8,9},{9,10},{10,1... | collective-permute-start | bytes 24584 | tf_op jit(solution)/shard_map/ppermute | solution.py:19
  73.8 3.3 %collective-permute-start.13 = (f32[4,1,512]{2,1,0:T(1,128)S(1)}, f32[4,1,512]{2,1,0:T(1,128)S(1)}, u32[]{:S(2)}, u32[]{:S(2)}) collective-permute-start(f32[4,1,512]{2,1,0:T(1,128)S(1)} %get-tuple-element.74), channel_id=1, source_target_pairs={{1,0},{2,1},{3,2},{4,3},{5,4},{6,5},{7,6},{8,7},{9,8},{10,9},{11,1... | collective-permute-start | bytes 24584 | tf_op jit(solution)/shard_map/ppermute | solution.py:21
  77.4 7.2 %collective-permute-start.14 = (f32[1,1,512]{2,1,0:T(1,128)S(1)}, f32[1,1,512]{2,1,0:T(1,128)S(1)}, u32[]{:S(2)}, u32[]{:S(2)}) collective-permute-start(f32[1,1,512]{2,1,0:T(1,128)S(1)} %get-tuple-element.91), channel_id=1, source_target_pairs={{0,1},{1,2},{2,3},{3,4},{4,5},{5,6},{6,7},{7,8},{8,9},{9,10},{10,1... | collective-permute-start | bytes 6152 | tf_op jit(solution)/shard_map/ppermute | solution.py:19
  83.3 3.1 %collective-permute-start.15 = (f32[1,1,512]{2,1,0:T(1,128)S(1)}, f32[1,1,512]{2,1,0:T(1,128)S(1)}, u32[]{:S(2)}, u32[]{:S(2)}) collective-permute-start(f32[1,1,512]{2,1,0:T(1,128)S(1)} %get-tuple-element.92), channel_id=1, source_target_pairs={{1,0},{2,1},{3,2},{4,3},{5,4},{6,5},{7,6},{8,7},{9,8},{10,9},{11,1... | collective-permute-start | bytes 6152 | tf_op jit(solution)/shard_map/ppermute | solution.py:21
  86.9 6.0 %collective-permute-start.16 = (f32[4,1,512]{2,1,0:T(1,128)S(1)}, f32[4,1,512]{2,1,0:T(1,128)S(1)}, u32[]{:S(2)}, u32[]{:S(2)}) collective-permute-start(f32[4,1,512]{2,1,0:T(1,128)S(1)} %get-tuple-element.71), channel_id=1, source_target_pairs={{0,1},{1,2},{2,3},{3,4},{4,5},{5,6},{6,7},{7,8},{8,9},{9,10},{10,1... | collective-permute-start | bytes 24584 | tf_op jit(solution)/shard_map/ppermute | solution.py:19
  91.6 3.1 %collective-permute-start.17 = (f32[4,1,512]{2,1,0:T(1,128)S(1)}, f32[4,1,512]{2,1,0:T(1,128)S(1)}, u32[]{:S(2)}, u32[]{:S(2)}) collective-permute-start(f32[4,1,512]{2,1,0:T(1,128)S(1)} %get-tuple-element.72), channel_id=1, source_target_pairs={{1,0},{2,1},{3,2},{4,3},{5,4},{6,5},{7,6},{8,7},{9,8},{10,9},{11,1... | collective-permute-start | bytes 24584 | tf_op jit(solution)/shard_map/ppermute | solution.py:21
  118.5 2.6 %collective-permute-start.18 = (f32[1,1,512]{2,1,0:T(1,128)S(1)}, f32[1,1,512]{2,1,0:T(1,128)S(1)}, u32[]{:S(2)}, u32[]{:S(2)}) collective-permute-start(f32[1,1,512]{2,1,0:T(1,128)S(1)} %get-tuple-element.89), channel_id=1, source_target_pairs={{0,1},{1,2},{2,3},{3,4},{4,5},{5,6},{6,7},{7,8},{8,9},{9,10},{10,1... | collective-permute-start | bytes 6152 | tf_op jit(solution)/shard_map/ppermute | solution.py:19
  119.8 3.7 %collective-permute-start.19 = (f32[1,1,512]{2,1,0:T(1,128)S(1)}, f32[1,1,512]{2,1,0:T(1,128)S(1)}, u32[]{:S(2)}, u32[]{:S(2)}) collective-permute-start(f32[1,1,512]{2,1,0:T(1,128)S(1)} %get-tuple-element.90), channel_id=1, source_target_pairs={{1,0},{2,1},{3,2},{4,3},{5,4},{6,5},{7,6},{8,7},{9,8},{10,9},{11,1... | collective-permute-start | bytes 6152 | tf_op jit(solution)/shard_map/ppermute | solution.py:21
  124.0 5.6 %collective-permute-start.20 = (f32[4,1,512]{2,1,0:T(1,128)S(1)}, f32[4,1,512]{2,1,0:T(1,128)S(1)}, u32[]{:S(2)}, u32[]{:S(2)}) collective-permute-start(f32[4,1,512]{2,1,0:T(1,128)S(1)} %get-tuple-element.69), channel_id=1, source_target_pairs={{0,1},{1,2},{2,3},{3,4},{4,5},{5,6},{6,7},{7,8},{8,9},{9,10},{10,1... | collective-permute-start | bytes 24584 | tf_op jit(solution)/shard_map/ppermute | solution.py:19
  128.3 3.1 %collective-permute-start.21 = (f32[4,1,512]{2,1,0:T(1,128)S(1)}, f32[4,1,512]{2,1,0:T(1,128)S(1)}, u32[]{:S(2)}, u32[]{:S(2)}) collective-permute-start(f32[4,1,512]{2,1,0:T(1,128)S(1)} %get-tuple-element.70), channel_id=1, source_target_pairs={{1,0},{2,1},{3,2},{4,3},{5,4},{6,5},{7,6},{8,7},{9,8},{10,9},{11,1... | collective-permute-start | bytes 24584 | tf_op jit(solution)/shard_map/ppermute | solution.py:21
  (4 other events, 24.2 us)
